TPU v7x, 32 devices: a whole 2x2x4 slice. The times are simulated.
32 devices in a mesh: dp: 16 (over z, y, x), mp: 2 (over core).
Axes of the slice: x: 2, y: 2, z: 4, core: 2. Of those that a mesh axis runs over, the one named last changes fastest.
Arguments:
- tokens: bfloat16 [512, 7168], P('dp', 'mp'), may hold values from -6 to 6
- gate_weight: bfloat16 [7168, 18432], P('mp', 'dp'), may hold values from -0.0625 to 0.0625
- up_weight: bfloat16 [7168, 18432], P('mp', 'dp'), may hold values from -0.0625 to 0.0625
- down_weight: bfloat16 [18432, 7168], P('dp', 'mp'), may hold values from -0.046875 to 0.046875
- gate_round: bfloat16 [7168, 18432], P('mp', 'dp'), may hold values from -8 to 8
- up_round: bfloat16 [7168, 18432], P('mp', 'dp'), may hold values from -8 to 8
- down_round: bfloat16 [18432, 7168], P('dp', 'mp'), may hold values from -8 to 8
- quant_scale: float32 [2, 18432], P(None, 'dp'), may hold values from 0.3 to 3
- quant_bits: int32 [2, 18432], P(None, 'dp'), may hold values from 2 to 4
- quant_zero: int32 [2, 18432], P(None, 'dp'), may hold values from 0 to 2
- down_scale: float32 [7168], P('mp'), may hold values from 0.3 to 3
- down_bits: int32 [7168], P('mp'), may hold values from 2 to 4
- down_zero: int32 [7168], P('mp'), may hold values from 0 to 2
- fisher: float32 [512], replicated, may hold values from 1 to 300, as said below
Outputs:
- loss_value: float32 [], replicated
- grad_gate: bfloat16 [7168, 18432], P('mp', 'dp')
- grad_up: bfloat16 [7168, 18432], P('mp', 'dp')
- grad_down: bfloat16 [18432, 7168], P('dp', 'mp')
Inputs may be any that keep to these rules, and one draw needn't show every extreme that they name: `fisher`: positive weights.
All inputs are finite; a program needn't handle non-finite values.
Results may differ from a plain program's by a relative error of at most 0.0059.
Values may be sent and summed in bfloat16 or wider, within the bound.
A program may use at most 192 MiB of HBM per device.

v0:
```python
import jax
import jax.numpy as jnp
from jax import lax
from jax.sharding import PartitionSpec as P

D = 7168
FF = 18432


def soft_weight(weight, variable, channel_scale, bit_width, zero_point, fan_in):
    quant_step = channel_scale / jnp.sqrt(jnp.float32(fan_in))
    offset = jnp.clip(1.2 * jax.nn.sigmoid(variable.astype(jnp.float32)) - 0.1, 0.0, 1.0)
    ceiling = (jnp.left_shift(jnp.int32(1), bit_width) - 1).astype(jnp.float32)
    zero_level = zero_point.astype(jnp.float32)
    levels = jnp.clip(
        weight.astype(jnp.float32) / quant_step + offset - 0.5 + zero_level, 0.0, ceiling
    )
    return (quant_step * (levels - zero_level)).astype(jnp.bfloat16)


def contract_rows(left, right):
    return lax.dot_general(
        left, right, (((0,), (0,)), ((), ())), preferred_element_type=jnp.float32
    )


def shards(
    tokens,
    gate_weight,
    up_weight,
    down_weight,
    gate_round,
    up_round,
    down_round,
    quant_scale,
    quant_bits,
    quant_zero,
    down_scale,
    down_bits,
    down_zero,
    fisher,
):
    own_rows = tokens.shape[0]
    hidden_cols = gate_weight.shape[1]
    all_tokens = lax.all_gather(tokens, "dp", axis=0, tiled=True)
    total_rows = all_tokens.shape[0]
    gate_student = soft_weight(
        gate_weight, gate_round, quant_scale[0], quant_bits[0], quant_zero[0], D
    )
    up_student = soft_weight(up_weight, up_round, quant_scale[1], quant_bits[1], quant_zero[1], D)
    stacked = jnp.concatenate([gate_weight, up_weight, gate_student, up_student], axis=1)
    partial_value = jnp.dot(all_tokens, stacked, preferred_element_type=jnp.float32)
    shares = lax.psum_scatter(partial_value, "mp", scatter_dimension=0, tiled=True)
    gate_teacher = shares[:, :hidden_cols]
    up_teacher = shares[:, hidden_cols : 2 * hidden_cols]
    gate_own = shares[:, 2 * hidden_cols : 3 * hidden_cols]
    up_own = shares[:, 3 * hidden_cols :]
    hidden_teacher = (jax.nn.silu(gate_teacher) * up_teacher).astype(jnp.bfloat16)
    hidden_student = (jax.nn.silu(gate_own) * up_own).astype(jnp.bfloat16)
    hidden = lax.all_gather(
        jnp.concatenate([hidden_teacher, hidden_student], axis=1), "mp", axis=0, tiled=True
    )
    down_student = soft_weight(down_weight, down_round, down_scale, down_bits, down_zero, FF)
    terms = jnp.dot(
        hidden,
        jnp.concatenate([-down_weight, down_student], axis=0),
        preferred_element_type=jnp.float32,
    )
    summed = lax.psum_scatter(terms, "dp", scatter_dimension=0, tiled=True)
    token_weight = lax.dynamic_slice_in_dim(fisher, lax.axis_index("dp") * own_rows, own_rows)
    weighted = token_weight[:, None] * summed
    partial_loss = jnp.sum(weighted * summed)
    local_grad = (2.0 * weighted).astype(jnp.bfloat16)
    loss_sum = lax.psum(partial_loss, ("dp", "mp"))
    out_grad = lax.all_gather(local_grad, "dp", axis=0, tiled=True)
    loss_value = loss_sum / (total_rows * D)
    grad_down = contract_rows(hidden[:, hidden_cols:], out_grad).astype(jnp.bfloat16)
    hidden_part = lax.dot_general(
        out_grad, down_student, (((1,), (1,)), ((), ())), preferred_element_type=jnp.float32
    )
    hidden_grad = lax.psum_scatter(hidden_part, "mp", scatter_dimension=0, tiled=True)
    sigmoid_gate = jax.nn.sigmoid(gate_own)
    gate_grad = (
        hidden_grad * up_own * sigmoid_gate * (1.0 + gate_own * (1.0 - sigmoid_gate))
    ).astype(jnp.bfloat16)
    up_grad = (hidden_grad * gate_own * sigmoid_gate).astype(jnp.bfloat16)
    both_grads = lax.all_gather(
        jnp.concatenate([gate_grad, up_grad], axis=1), "mp", axis=0, tiled=True
    )
    weight_grads = contract_rows(all_tokens, both_grads)
    grad_gate = weight_grads[:, :hidden_cols].astype(jnp.bfloat16)
    grad_up = weight_grads[:, hidden_cols:].astype(jnp.bfloat16)
    return (loss_value, grad_gate, grad_up, grad_down)


def solution(mesh):
    in_specs = (
        P("dp", "mp"),
        P("mp", "dp"),
        P("mp", "dp"),
        P("dp", "mp"),
        P("mp", "dp"),
        P("mp", "dp"),
        P("dp", "mp"),
        P(None, "dp"),
        P(None, "dp"),
        P(None, "dp"),
        P("mp"),
        P("mp"),
        P("mp"),
        P(),
    )
    out_specs = (P(), P("mp", "dp"), P("mp", "dp"), P("dp", "mp"))
    return jax.shard_map(shards, mesh=mesh, in_specs=in_specs, out_specs=out_specs, check_vma=False)
```

profile of v0, /device:TPU:0, one launch (start us, length us, event | category | flops | bytes accessed | tf_op | source)
XLA Modules:
  0.0 532.8 jit_solution(1226961479305919175)
XLA Ops:
  8.8 0.8 convert_reduce_fusion.3
  9.6 0.8 multiply_reduce_fusion.1
  10.4 24.4 %multiply_convert_fusion.1 = (bf16[3584,1152]{1,0:T(8,128)(2,1)}, bf16[3584,1152]{1,0:T(8,128)(2,1)}) fusion(bf16[3584,1152]{1,0:T(8,128)(2,1)} %param.19, bf16[3584,1152]{1,0:T(8,128)(2,1)} %param.16, f32[1152]{0:T(1024)S(1)} %get-tuple-element.13, f32[1152]{0:T(1024)S(1)} %get-tuple-element.11, f32[1152]{0:T(1024)S(1)} %get-tuple-element.9, ...), kind=kLoop, calls=%fused_computation.15 | loop fusion | flops 140378112 | bytes 49572864 | tf_op jit(solution)/shard_map/convert_element_type | solution.py:18
  34.7 50.4 %all-gather.5.cloned.1.call-done = bf16[512,3584]{1,0:T(8,128)(2,1)} async-done(((bf16[32,3584]{1,0:T(8,128)(2,1)}), bf16[512,3584]{1,0:T(8,128)(2,1)}) %all-gather.5.cloned.1.call-update) | async-done | bytes 3670032 | tf_op jit(solution)/shard_map/all_gather | solution.py:45
  85.1 25.0 %fusion.13 = f32[512,4608]{0,1:T(8,128)} fusion(bf16[512,3584]{1,0:T(8,128)(2,1)} %all-gather.5.cloned.1.call-done, bf16[3584,1152]{1,0:T(8,128)(2,1)} %get-tuple-element.22, bf16[3584,1152]{1,0:T(8,128)(2,1)} %get-tuple-element.23, bf16[3584,1152]{1,0:T(8,128)(2,1)} %param.16, bf16[3584,1152]{1,0:T(8,128)(2,1)} %param.15), kind=kOutput, calls=%fused_computation.18 | convolution fusion | flops 17043554304 | bytes 46137344 | tf_op jit(solution)/shard_map/dot_general | solution.py:52
  110.9 15.0 %reduce-scatter.4.cloned.1.call-done = f32[256,4608]{0,1:T(8,128)} async-done(((f32[512,4608]{0,1:T(8,128)}), f32[256,4608]{0,1:T(8,128)}) %reduce-scatter.4.cloned.1.call-update) | async-done | bytes 4718608 | tf_op jit(solution)/shard_map/reduce_scatter | solution.py:53
  125.9 3.0 fusion.17
  128.9 1.1 pad_maximum_fusion
  130.2 14.3 %multiply_convert_fusion = bf16[1152,3584]{1,0:T(8,128)(2,1)} fusion(bf16[1152,3584]{1,0:T(8,128)(2,1)} %param.20, bf16[1152,3584]{1,0:T(8,128)(2,1)} %param.17, f32[3584]{0:T(1024)S(1)} %convert_element_type.84, f32[3584]{0:T(1024)S(1)} %add_convert_fusion, f32[3584]{0:T(1024)S(1)} %broadcast_multiply_fusion), kind=kLoop, calls=%fused_computation.14 | loop fusion | flops 70189056 | bytes 24815616 | tf_op jit(solution)/shard_map/convert_element_type | solution.py:18
  144.5 8.2 %neg.24 = bf16[1152,3584]{1,0:T(8,128)(2,1)} negate(bf16[1152,3584]{1,0:T(8,128)(2,1)} %param.17) | non-fusion elementwise | flops 4128768 | bytes 16515072 | tf_op jit(solution)/shard_map/neg | solution.py:66
  152.7 15.0 %fusion.9 = f32[512,3584]{1,0:T(8,128)} fusion(bf16[512,2304]{0,1:T(8,128)(2,1)} %all-gather.7.cloned.1.call-done, bf16[1152,3584]{1,0:T(8,128)(2,1)} %multiply_convert_fusion, bf16[1152,3584]{1,0:T(8,128)(2,1)} %neg.24), kind=kOutput, calls=%fused_computation.10 | convolution fusion | flops 8488747008 | bytes 26214400 | tf_op jit(solution)/shard_map/dot_general | solution.py:64
  168.5 157.4 %reduce-scatter.6.cloned.1.call-done = f32[32,3584]{1,0:T(8,128)} async-done(((f32[512,3584]{1,0:T(8,128)}), f32[32,3584]{1,0:T(8,128)}) %reduce-scatter.6.cloned.1.call-update) | async-done | bytes 458768 | tf_op jit(solution)/shard_map/reduce_scatter | solution.py:69
  326.0 2.4 fusion.19
  328.5 74.7 %all-gather.9.cloned.1.call-done = bf16[512,3584]{1,0:T(8,128)(2,1)} async-done(((bf16[32,3584]{1,0:T(8,128)(2,1)}), bf16[512,3584]{1,0:T(8,128)(2,1)}) %all-gather.9.cloned.1.call-update) | async-done | bytes 3670032 | tf_op jit(solution)/shard_map/all_gather | solution.py:75
  403.2 10.3 %fusion.23 = f32[512,1152]{0,1:T(8,128)} fusion(bf16[512,3584]{1,0:T(8,128)(2,1)} %all-gather.9.cloned.1.call-done, bf16[1152,3584]{1,0:T(8,128)(2,1)} %multiply_convert_fusion), kind=kOutput, calls=%fused_computation.43 | convolution fusion | flops 4227858432 | bytes 14286848 | tf_op jit(solution)/shard_map/dot_general | solution.py:78
  413.8 8.4 %reduce-scatter.8.cloned.1.call-done = f32[256,1152]{0,1:T(8,128)} async-done(((f32[512,1152]{0,1:T(8,128)}), f32[256,1152]{0,1:T(8,128)}) %reduce-scatter.8.cloned.1.call-update) | async-done | bytes 1179664 | tf_op jit(solution)/shard_map/reduce_scatter | solution.py:81
  422.2 2.5 multiply_convert_fusion.4
  424.7 1.1 pad_maximum_fusion.1
  425.8 40.9 %psum.7 = f32[]{:T(128)} all-reduce(f32[]{:T(128)} %get-tuple-element.21), channel_id=1, replica_groups=mesh['dp'=16,'mp'=2] {'dp','mp'}, use_global_device_ids=true, to_apply=%region_3.4 | all-reduce | flops 1 | bytes 8 | tf_op jit(solution)/shard_map/psum | solution.py:74
  467.3 8.7 %convolution_convert_fusion.1 = bf16[1152,3584]{1,0:T(8,128)(2,1)} fusion(bf16[512,3584]{1,0:T(8,128)(2,1)} %all-gather.9.cloned.1.call-done, bf16[512,2304]{0,1:T(8,128)(2,1)S(1)} %copy-done.3), kind=kOutput, calls=%fused_computation.17 | convolution fusion | flops 4231987200 | bytes 13107200 | tf_op jit(solution)/shard_map/dot_general | solution.py:22
  476.0 14.4 %fusion.8 = bf16[3584,2304]{0,1:T(8,128)(2,1)} fusion(bf16[512,2304]{0,1:T(8,128)(2,1)} %all-gather.11.cloned.1.call-done, bf16[512,3584]{1,0:T(8,128)(2,1)} %all-gather.5.cloned.1.call-done), kind=kOutput, calls=%fused_computation.9 | convolution fusion | flops 8463974400 | bytes 22544384 | tf_op jit(solution)/shard_map/dot_general | solution.py:22
  490.4 11.4 %fusion.22 = (bf16[3584,1152]{0,1:T(8,128)(2,1)}, bf16[3584,1152]{0,1:T(8,128)(2,1)}) fusion(bf16[3584,2304]{0,1:T(8,128)(2,1)} %fusion.8), kind=kLoop, calls=%fused_computation.42 | loop fusion | bytes 33030144 | tf_op jit(solution)/shard_map/slice | solution.py:92
  501.8 11.5 %copy.19 = bf16[3584,1152]{1,0:T(8,128)(2,1)} copy(bf16[3584,1152]{0,1:T(8,128)(2,1)} %get-tuple-element.15) | data formatting | bytes 16515072
  513.3 11.5 %copy.20 = bf16[3584,1152]{1,0:T(8,128)(2,1)} copy(bf16[3584,1152]{0,1:T(8,128)(2,1)} %get-tuple-element.14) | data formatting | bytes 16515072
  (29 shorter events, 3.7 us)
Async XLA Ops:
  7.2 77.9 %all-gather.5.cloned.1.call-start = ((), (), s32[]{:S(2)}) async-start(), calls=%async_computation.3 | async-start | bytes 3899392 | tf_op jit(solution)/shard_map/all_gather | solution.py:45
  7.9 118.0 %reduce-scatter.4.cloned.1.call-start = ((), (), s32[]{:S(2)}) async-start(), calls=%async_computation.4 | async-start | bytes 14155776 | tf_op jit(solution)/shard_map/reduce_scatter | solution.py:53
  110.1 0.7 copy-start
  110.1 0.7 copy-start.1
  110.1 0.7 copy-start.2
  110.1 42.5 %all-gather.7.cloned.1.call-start = ((), (), s32[]{:S(2)}) async-start(), calls=%async_computation.5 | async-start | bytes 3538944 | tf_op jit(solution)/shard_map/all_gather | solution.py:60
  130.0 196.0 %reduce-scatter.6.cloned.1.call-start = ((), (), s32[]{:S(2)}) async-start(), calls=%async_computation.6 | async-start | bytes 7798784 | tf_op jit(solution)/shard_map/reduce_scatter | solution.py:69
  167.7 235.5 %all-gather.9.cloned.1.call-start = ((), (), s32[]{:S(2)}) async-start(), calls=%async_computation.7 | async-start | bytes 3899392 | tf_op jit(solution)/shard_map/all_gather | solution.py:75
  328.4 93.8 %reduce-scatter.8.cloned.1.call-start = ((), (), s32[]{:S(2)}) async-start(), calls=%async_computation.8 | async-start | bytes 3538944 | tf_op jit(solution)/shard_map/reduce_scatter | solution.py:81
  413.5 53.8 %copy-start.3 = (bf16[512,2304]{0,1:T(8,128)(2,1)S(1)}, bf16[512,2304]{0,1:T(8,128)(2,1)}, u32[]{:S(2)}) copy-start(bf16[512,2304]{0,1:T(8,128)(2,1)} %all-gather.7.cloned.1.call-done) | copy-start | bytes 7077892
  413.6 62.5 %all-gather.11.cloned.1.call-start = ((), (), s32[]{:S(2)}) async-start(), calls=%async_computation.9 | async-start | bytes 3538944 | tf_op jit(solution)/shard_map/all_gather | solution.py:87
Sparse Core Ops, SparseCore 0:
  10.7 74.3 all-gather.4
  110.3 15.5 reduce-scatter.3
  130.1 11.7 all-gather.6
  167.8 158.0 reduce-scatter.5
  329.1 73.9 all-gather.8
  413.7 8.4 reduce-scatter.7
  426.0 11.7 all-gather.10
where the time goes:
time: 534 us; the launch traced here: 533 us
  waiting for transfers between devices  307 us (57%)
  matrix products  73.5 us (14%)
  other arithmetic  59.4 us (11%)
  blocking collectives  40.9 us (8%)
  local copies, waits for them, and re-layouts  35.8 us (7%)
  between operations  16 us (3%)
    reduce_scatter x1, waiting for transfers between devices, shards(): summed = lax.psum_scatter(terms, 'dp', scatter_dimension=0, tiled=True)  157 us
    all_gather x1, waiting for transfers between devices, shards(): out_grad = lax.all_gather(local_grad, 'dp', axis=0, tiled=True)  74.7 us
    all_gather x1, waiting for transfers between devices, shards(): all_tokens = lax.all_gather(tokens, 'dp', axis=0, tiled=True)  50.4 us
    psum x1, blocking collectives, shards(): loss_sum = lax.psum(partial_loss, ('dp', 'mp'))  40.9 us
    convert_element_type x2, other arithmetic, soft_weight(): return (quant_step * (levels - zero_level)).astype(jnp.bfloat16)  38.6 us
    dot_general x1, matrix products, shards(): jnp.dot(all_tokens, stacked, preferred_element_type=jnp.float32)  25 us
    unnamed x10, local copies, waits for them, and re-layouts  23.7 us
    dot_general x2, matrix products, contract_rows(): lax.dot_general(left, right, (((0,), (0,)), ((), ())), preferred_element_...  23.1 us
  transfers between devices with their start and end apart: 7, of which 5 were waited for; matrix products, arithmetic and copies ran while one was open for 11% of the time, Pallas kernels for 0%

commit v1 on v0

--- a/solution.py
+++ b/solution.py
@@ -42,7 +42,12 @@
 ):
     own_rows = tokens.shape[0]
     hidden_cols = gate_weight.shape[1]
-    all_tokens = lax.all_gather(tokens, "dp", axis=0, tiled=True)
+    ring = [tokens]
+    for hop in range(15):
+        ring.append(lax.ppermute(ring[-1], "dp", [(dev, (dev + 1) % 16) for dev in range(16)]))
+    all_tokens = jnp.roll(
+        jnp.concatenate(ring[::-1], axis=0), (lax.axis_index("dp") + 1) * ring[0].shape[0], axis=0
+    )
     total_rows = all_tokens.shape[0]
     gate_student = soft_weight(
         gate_weight, gate_round, quant_scale[0], quant_bits[0], quant_zero[0], D

time: 534 us -> 634 us (1.19)
  waiting for transfers between devices: 307 us -> 398 us
  matrix products: 73.5 us -> 81.9 us
    ppermute x0 -> x15, waiting for transfers between devices: none -> 139 us  [shards(): lax.ppermute(ring[-1], 'dp', [(dev, (dev + 1) % 16) for dev in range(16)])]
    all_gather x1 -> x0, waiting for transfers between devices: 50.4 us -> none  [shards(): all_tokens = lax.all_gather(tokens, 'dp', axis=0, tiled=True)]
    dot_general x1, matrix products: 25 us -> 33.4 us  [shards(): jnp.dot(all_tokens, stacked, preferred_element_type=jnp.float32)]
    unnamed x10 -> x67, local copies, waits for them, and re-layouts: 23.7 us -> 18.4 us
  transfers between devices with their start and end apart: 7 -> 21, of which waited for: 5 -> 18; matrix products, arithmetic and copies ran while one was open for 11% -> 9% of each run, Pallas kernels for 0% -> 0%
where the time goes in v1:
time: 634 us; the launch traced here: 633 us
  waiting for transfers between devices  398 us (63%)
  matrix products  81.9 us (13%)
  other arithmetic  59.3 us (9%)
  blocking collectives  41.1 us (6%)
  local copies, waits for them, and re-layouts  32.8 us (5%)
  between operations  16.3 us (3%)
    reduce_scatter x1, waiting for transfers between devices, shards(): summed = lax.psum_scatter(terms, 'dp', scatter_dimension=0, tiled=True)  157 us
    ppermute x15, waiting for transfers between devices, shards(): lax.ppermute(ring[-1], 'dp', [(dev, (dev + 1) % 16) for dev in range(16)])  139 us
    all_gather x1, waiting for transfers between devices, shards(): out_grad = lax.all_gather(local_grad, 'dp', axis=0, tiled=True)  74.7 us
    psum x1, blocking collectives, shards(): loss_sum = lax.psum(partial_loss, ('dp', 'mp'))  41.1 us
    convert_element_type x2, other arithmetic, soft_weight(): return (quant_step * (levels - zero_level)).astype(jnp.bfloat16)  38.4 us
    dot_general x1, matrix products, shards(): jnp.dot(all_tokens, stacked, preferred_element_type=jnp.float32)  33.4 us
    dot_general x2, matrix products, contract_rows(): lax.dot_general(left, right, (((0,), (0,)), ((), ())), preferred_element_...  22.9 us
    unnamed x67, local copies, waits for them, and re-layouts  18.4 us
  transfers between devices with their start and end apart: 21, of which 18 were waited for; matrix products, arithmetic and copies ran while one was open for 9% of the time, Pallas kernels for 0%

profile of v1, /device:TPU:0, one launch (start us, length us, event | category | flops | bytes accessed | tf_op | source)
XLA Modules:
  0.0 632.8 jit_solution(673930618076973902)
XLA Ops:
  10.2 9.8 %collective-permute-done = bf16[32,3584]{1,0:T(8,128)(2,1)S(1)} collective-permute-done((bf16[32,3584]{1,0:T(8,128)(2,1)}, bf16[32,3584]{1,0:T(8,128)(2,1)S(1)}, u32[]{:S(2)}, u32[]{:S(2)}) %collective-permute-start) | collective-permute-done | bytes 229408 | tf_op jit(solution)/shard_map/ppermute | solution.py:47
  20.0 10.4 %collective-permute-done.1 = bf16[32,3584]{1,0:T(8,128)(2,1)S(1)} collective-permute-done((bf16[32,3584]{1,0:T(8,128)(2,1)S(1)}, bf16[32,3584]{1,0:T(8,128)(2,1)S(1)}, u32[]{:S(2)}, u32[]{:S(2)}) %collective-permute-start.1) | collective-permute-done | bytes 229408 | tf_op jit(solution)/shard_map/ppermute | solution.py:47
  30.4 9.6 %collective-permute-done.2 = bf16[32,3584]{1,0:T(8,128)(2,1)S(1)} collective-permute-done((bf16[32,3584]{1,0:T(8,128)(2,1)S(1)}, bf16[32,3584]{1,0:T(8,128)(2,1)S(1)}, u32[]{:S(2)}, u32[]{:S(2)}) %collective-permute-start.2) | collective-permute-done | bytes 229408 | tf_op jit(solution)/shard_map/ppermute | solution.py:47
  40.0 9.6 %collective-permute-done.3 = bf16[32,3584]{1,0:T(8,128)(2,1)S(1)} collective-permute-done((bf16[32,3584]{1,0:T(8,128)(2,1)S(1)}, bf16[32,3584]{1,0:T(8,128)(2,1)S(1)}, u32[]{:S(2)}, u32[]{:S(2)}) %collective-permute-start.3) | collective-permute-done | bytes 229408 | tf_op jit(solution)/shard_map/ppermute | solution.py:47
  49.6 9.6 %collective-permute-done.4 = bf16[32,3584]{1,0:T(8,128)(2,1)S(1)} collective-permute-done((bf16[32,3584]{1,0:T(8,128)(2,1)S(1)}, bf16[32,3584]{1,0:T(8,128)(2,1)S(1)}, u32[]{:S(2)}, u32[]{:S(2)}) %collective-permute-start.4) | collective-permute-done | bytes 229408 | tf_op jit(solution)/shard_map/ppermute | solution.py:47
  59.3 9.6 %collective-permute-done.5 = bf16[32,3584]{1,0:T(8,128)(2,1)S(1)} collective-permute-done((bf16[32,3584]{1,0:T(8,128)(2,1)S(1)}, bf16[32,3584]{1,0:T(8,128)(2,1)S(1)}, u32[]{:S(2)}, u32[]{:S(2)}) %collective-permute-start.5) | collective-permute-done | bytes 229408 | tf_op jit(solution)/shard_map/ppermute | solution.py:47
  68.9 10.8 %collective-permute-done.6 = bf16[32,3584]{1,0:T(8,128)(2,1)S(1)} collective-permute-done((bf16[32,3584]{1,0:T(8,128)(2,1)S(1)}, bf16[32,3584]{1,0:T(8,128)(2,1)S(1)}, u32[]{:S(2)}, u32[]{:S(2)}) %collective-permute-start.6) | collective-permute-done | bytes 229408 | tf_op jit(solution)/shard_map/ppermute | solution.py:47
  79.6 11.9 %collective-permute-done.7 = bf16[32,3584]{1,0:T(8,128)(2,1)S(1)} collective-permute-done((bf16[32,3584]{1,0:T(8,128)(2,1)S(1)}, bf16[32,3584]{1,0:T(8,128)(2,1)S(1)}, u32[]{:S(2)}, u32[]{:S(2)}) %collective-permute-start.7) | collective-permute-done | bytes 229408 | tf_op jit(solution)/shard_map/ppermute | solution.py:47
  91.6 11.2 %collective-permute-done.8 = bf16[32,3584]{1,0:T(8,128)(2,1)S(1)} collective-permute-done((bf16[32,3584]{1,0:T(8,128)(2,1)S(1)}, bf16[32,3584]{1,0:T(8,128)(2,1)S(1)}, u32[]{:S(2)}, u32[]{:S(2)}) %collective-permute-start.8) | collective-permute-done | bytes 229408 | tf_op jit(solution)/shard_map/ppermute | solution.py:47
  102.8 10.4 %collective-permute-done.9 = bf16[32,3584]{1,0:T(8,128)(2,1)S(1)} collective-permute-done((bf16[32,3584]{1,0:T(8,128)(2,1)S(1)}, bf16[32,3584]{1,0:T(8,128)(2,1)S(1)}, u32[]{:S(2)}, u32[]{:S(2)}) %collective-permute-start.9) | collective-permute-done | bytes 229408 | tf_op jit(solution)/shard_map/ppermute | solution.py:47
  113.1 9.6 %collective-permute-done.10 = bf16[32,3584]{1,0:T(8,128)(2,1)S(1)} collective-permute-done((bf16[32,3584]{1,0:T(8,128)(2,1)S(1)}, bf16[32,3584]{1,0:T(8,128)(2,1)S(1)}, u32[]{:S(2)}, u32[]{:S(2)}) %collective-permute-start.10) | collective-permute-done | bytes 229408 | tf_op jit(solution)/shard_map/ppermute | solution.py:47
  122.8 9.6 %collective-permute-done.11 = bf16[32,3584]{1,0:T(8,128)(2,1)S(1)} collective-permute-done((bf16[32,3584]{1,0:T(8,128)(2,1)S(1)}, bf16[32,3584]{1,0:T(8,128)(2,1)S(1)}, u32[]{:S(2)}, u32[]{:S(2)}) %collective-permute-start.11) | collective-permute-done | bytes 229408 | tf_op jit(solution)/shard_map/ppermute | solution.py:47
  132.4 9.6 %collective-permute-done.12 = bf16[32,3584]{1,0:T(8,128)(2,1)S(1)} collective-permute-done((bf16[32,3584]{1,0:T(8,128)(2,1)S(1)}, bf16[32,3584]{1,0:T(8,128)(2,1)S(1)}, u32[]{:S(2)}, u32[]{:S(2)}) %collective-permute-start.12) | collective-permute-done | bytes 229408 | tf_op jit(solution)/shard_map/ppermute | solution.py:47
  151.7 24.2 %multiply_convert_fusion.1 = (bf16[3584,1152]{1,0:T(8,128)(2,1)}, bf16[3584,1152]{1,0:T(8,128)(2,1)}) fusion(bf16[3584,1152]{1,0:T(8,128)(2,1)} %param.19, bf16[3584,1152]{1,0:T(8,128)(2,1)} %param.16, f32[1152]{0:T(1024)S(1)} %get-tuple-element.9, f32[1152]{0:T(1024)S(1)} %get-tuple-element.7, f32[1152]{0:T(1024)S(1)} %get-tuple-element.5, ...), kind=kLoop, calls=%fused_computation.14 | loop fusion | flops 140378112 | bytes 49572864 | tf_op jit(solution)/shard_map/convert_element_type | solution.py:18
  196.3 33.4 %fusion = f32[512,4608]{1,0:T(8,128)} fusion(bf16[3584,1152]{1,0:T(8,128)(2,1)} %get-tuple-element.18, bf16[3584,1152]{1,0:T(8,128)(2,1)} %get-tuple-element.19, bf16[3584,1152]{1,0:T(8,128)(2,1)S(1)} %bitcast.7, bf16[3584,1152]{1,0:T(8,128)(2,1)S(1)} %copy-done, bf16[512,3584]{1,0:T(8,128)(2,1)} %fusion.35), kind=kOutput, calls=%fused_computation | convolution fusion | flops 17043554304 | bytes 46137344 | tf_op jit(solution)/shard_map/dot_general | solution.py:57
  230.4 18.0 %reduce-scatter.4.cloned.1.call-done = f32[256,4608]{1,0:T(8,128)} async-done(((f32[512,4608]{1,0:T(8,128)}), f32[256,4608]{1,0:T(8,128)}) %reduce-scatter.4.cloned.1.call-update) | async-done | bytes 4718608 | tf_op jit(solution)/shard_map/reduce_scatter | solution.py:58
  252.7 14.2 %multiply_convert_fusion = bf16[1152,3584]{1,0:T(8,128)(2,1)} fusion(bf16[1152,3584]{1,0:T(8,128)(2,1)} %param.20, bf16[1152,3584]{1,0:T(8,128)(2,1)} %param.17, f32[3584]{0:T(1024)S(1)} %convert_element_type.84, f32[3584]{0:T(1024)S(1)} %add_convert_fusion, f32[3584]{0:T(1024)S(1)} %broadcast_multiply_fusion), kind=kLoop, calls=%fused_computation.13 | loop fusion | flops 70189056 | bytes 24815616 | tf_op jit(solution)/shard_map/convert_element_type | solution.py:18
  275.1 14.8 %fusion.8 = f32[512,3584]{1,0:T(8,128)} fusion(bf16[512,2304]{1,0:T(8,128)(2,1)} %all-gather.4.cloned.1.call-done, bf16[1152,3584]{1,0:T(8,128)(2,1)} %multiply_convert_fusion, bf16[1152,3584]{1,0:T(8,128)(2,1)} %neg.24), kind=kOutput, calls=%fused_computation.9 | convolution fusion | flops 8488747008 | bytes 26214400 | tf_op jit(solution)/shard_map/dot_general | solution.py:69
  290.7 157.4 %reduce-scatter.6.cloned.1.call-done = f32[32,3584]{1,0:T(8,128)} async-done(((f32[512,3584]{1,0:T(8,128)}), f32[32,3584]{1,0:T(8,128)}) %reduce-scatter.6.cloned.1.call-update) | async-done | bytes 458768 | tf_op jit(solution)/shard_map/reduce_scatter | solution.py:74
  450.7 74.7 %all-gather.6.cloned.1.call-done = bf16[512,3584]{1,0:T(8,128)(2,1)} async-done(((bf16[32,3584]{1,0:T(8,128)(2,1)}), bf16[512,3584]{1,0:T(8,128)(2,1)}) %all-gather.6.cloned.1.call-update) | async-done | bytes 3670032 | tf_op jit(solution)/shard_map/all_gather | solution.py:80
  525.4 10.8 %fusion.23 = f32[512,1152]{1,0:T(8,128)} fusion(bf16[512,3584]{1,0:T(8,128)(2,1)} %all-gather.6.cloned.1.call-done, bf16[1152,3584]{1,0:T(8,128)(2,1)} %multiply_convert_fusion), kind=kOutput, calls=%fused_computation.77 | convolution fusion | flops 4227858432 | bytes 14286848 | tf_op jit(solution)/shard_map/dot_general | solution.py:83
  548.6 41.1 %psum.7 = f32[]{:T(128)} all-reduce(f32[]{:T(128)} %get-tuple-element.17), channel_id=1, replica_groups=mesh['dp'=16,'mp'=2] {'dp','mp'}, use_global_device_ids=true, to_apply=%region_3.4 | all-reduce | flops 1 | bytes 8 | tf_op jit(solution)/shard_map/psum | solution.py:79
  598.9 14.4 %convolution_convert_fusion = bf16[3584,2304]{1,0:T(8,128)(2,1)} fusion(bf16[512,2304]{1,0:T(8,128)(2,1)} %all-gather.8.cloned.1.call-done, bf16[1024,3584]{1,0:T(8,128)(2,1)} %copy-done.1, s32[]{:T(128)S(6)} %select_n.18), kind=kOutput, calls=%fused_computation.8 | convolution fusion | flops 8463974400 | bytes 22544388 | tf_op jit(solution)/shard_map/dot_general | solution.py:22
  613.3 11.5 %fusion.22 = (bf16[3584,1152]{1,0:T(8,128)(2,1)}, bf16[3584,1152]{1,0:T(8,128)(2,1)}) fusion(bf16[3584,2304]{1,0:T(8,128)(2,1)} %convolution_convert_fusion), kind=kLoop, calls=%fused_computation.76 | loop fusion | bytes 33030144 | tf_op jit(solution)/shard_map/slice | solution.py:97
  (116 shorter events, 70.2 us)
Async XLA Ops:
  7.2 241.3 %reduce-scatter.4.cloned.1.call-start = ((), (), s32[]{:S(2)}) async-start(), calls=%async_computation.3 | async-start | bytes 14155776 | tf_op jit(solution)/shard_map/reduce_scatter | solution.py:58
  7.2 12.8 %collective-permute-start = (bf16[32,3584]{1,0:T(8,128)(2,1)}, bf16[32,3584]{1,0:T(8,128)(2,1)S(1)}, u32[]{:S(2)}, u32[]{:S(2)}) collective-permute-start(bf16[32,3584]{1,0:T(8,128)(2,1)} %param.14), channel_id=1, source_target_pairs={{0,2},{2,4},{4,6},{6,8},{8,10},{10,12},{12,14},{14,16},{16,18},{18... | collective-permute-start | bytes 688136 | tf_op jit(solution)/shard_map/ppermute | solution.py:47
  20.0 10.4 %collective-permute-start.1 = (bf16[32,3584]{1,0:T(8,128)(2,1)S(1)}, bf16[32,3584]{1,0:T(8,128)(2,1)S(1)}, u32[]{:S(2)}, u32[]{:S(2)}) collective-permute-start(bf16[32,3584]{1,0:T(8,128)(2,1)S(1)} %collective-permute-done), channel_id=1, source_target_pairs={{0,2},{2,4},{4,6},{6,8},{8,10},{10,12},{12,14},{14,16},{16,18},{18... | collective-permute-start | bytes 688136 | tf_op jit(solution)/shard_map/ppermute | solution.py:47
  30.4 9.6 %collective-permute-start.2 = (bf16[32,3584]{1,0:T(8,128)(2,1)S(1)}, bf16[32,3584]{1,0:T(8,128)(2,1)S(1)}, u32[]{:S(2)}, u32[]{:S(2)}) collective-permute-start(bf16[32,3584]{1,0:T(8,128)(2,1)S(1)} %collective-permute-done.1), channel_id=1, source_target_pairs={{0,2},{2,4},{4,6},{6,8},{8,10},{10,12},{12,14},{14,16},{16,18},{18... | collective-permute-start | bytes 688136 | tf_op jit(solution)/shard_map/ppermute | solution.py:47
  40.0 9.6 %collective-permute-start.3 = (bf16[32,3584]{1,0:T(8,128)(2,1)S(1)}, bf16[32,3584]{1,0:T(8,128)(2,1)S(1)}, u32[]{:S(2)}, u32[]{:S(2)}) collective-permute-start(bf16[32,3584]{1,0:T(8,128)(2,1)S(1)} %collective-permute-done.2), channel_id=1, source_target_pairs={{0,2},{2,4},{4,6},{6,8},{8,10},{10,12},{12,14},{14,16},{16,18},{18... | collective-permute-start | bytes 688136 | tf_op jit(solution)/shard_map/ppermute | solution.py:47
  49.6 9.6 %collective-permute-start.4 = (bf16[32,3584]{1,0:T(8,128)(2,1)S(1)}, bf16[32,3584]{1,0:T(8,128)(2,1)S(1)}, u32[]{:S(2)}, u32[]{:S(2)}) collective-permute-start(bf16[32,3584]{1,0:T(8,128)(2,1)S(1)} %collective-permute-done.3), channel_id=1, source_target_pairs={{0,2},{2,4},{4,6},{6,8},{8,10},{10,12},{12,14},{14,16},{16,18},{18... | collective-permute-start | bytes 688136 | tf_op jit(solution)/shard_map/ppermute | solution.py:47
  59.3 118.9 %copy-start.3 = (bf16[32,3584]{1,0:T(8,128)(2,1)}, bf16[32,3584]{1,0:T(8,128)(2,1)S(1)}, u32[]{:S(2)}) copy-start(bf16[32,3584]{1,0:T(8,128)(2,1)S(1)} %collective-permute-done.4) | copy-start | bytes 688132
  59.3 9.6 %collective-permute-start.5 = (bf16[32,3584]{1,0:T(8,128)(2,1)S(1)}, bf16[32,3584]{1,0:T(8,128)(2,1)S(1)}, u32[]{:S(2)}, u32[]{:S(2)}) collective-permute-start(bf16[32,3584]{1,0:T(8,128)(2,1)S(1)} %collective-permute-done.4), channel_id=1, source_target_pairs={{0,2},{2,4},{4,6},{6,8},{8,10},{10,12},{12,14},{14,16},{16,18},{18... | collective-permute-start | bytes 688136 | tf_op jit(solution)/shard_map/ppermute | solution.py:47
  68.9 109.3 %copy-start.4 = (bf16[32,3584]{1,0:T(8,128)(2,1)}, bf16[32,3584]{1,0:T(8,128)(2,1)S(1)}, u32[]{:S(2)}) copy-start(bf16[32,3584]{1,0:T(8,128)(2,1)S(1)} %collective-permute-done.5) | copy-start | bytes 688132
  68.9 10.8 %collective-permute-start.6 = (bf16[32,3584]{1,0:T(8,128)(2,1)S(1)}, bf16[32,3584]{1,0:T(8,128)(2,1)S(1)}, u32[]{:S(2)}, u32[]{:S(2)}) collective-permute-start(bf16[32,3584]{1,0:T(8,128)(2,1)S(1)} %collective-permute-done.5), channel_id=1, source_target_pairs={{0,2},{2,4},{4,6},{6,8},{8,10},{10,12},{12,14},{14,16},{16,18},{18... | collective-permute-start | bytes 688136 | tf_op jit(solution)/shard_map/ppermute | solution.py:47
  79.6 98.5 %copy-start.5 = (bf16[32,3584]{1,0:T(8,128)(2,1)}, bf16[32,3584]{1,0:T(8,128)(2,1)S(1)}, u32[]{:S(2)}) copy-start(bf16[32,3584]{1,0:T(8,128)(2,1)S(1)} %collective-permute-done.6) | copy-start | bytes 688132
  79.6 11.9 %collective-permute-start.7 = (bf16[32,3584]{1,0:T(8,128)(2,1)S(1)}, bf16[32,3584]{1,0:T(8,128)(2,1)S(1)}, u32[]{:S(2)}, u32[]{:S(2)}) collective-permute-start(bf16[32,3584]{1,0:T(8,128)(2,1)S(1)} %collective-permute-done.6), channel_id=1, source_target_pairs={{0,2},{2,4},{4,6},{6,8},{8,10},{10,12},{12,14},{14,16},{16,18},{18... | collective-permute-start | bytes 688136 | tf_op jit(solution)/shard_map/ppermute | solution.py:47
  91.6 11.2 %collective-permute-start.8 = (bf16[32,3584]{1,0:T(8,128)(2,1)S(1)}, bf16[32,3584]{1,0:T(8,128)(2,1)S(1)}, u32[]{:S(2)}, u32[]{:S(2)}) collective-permute-start(bf16[32,3584]{1,0:T(8,128)(2,1)S(1)} %collective-permute-done.7), channel_id=1, source_target_pairs={{0,2},{2,4},{4,6},{6,8},{8,10},{10,12},{12,14},{14,16},{16,18},{18... | collective-permute-start | bytes 688136 | tf_op jit(solution)/shard_map/ppermute | solution.py:47
  102.8 10.4 %collective-permute-start.9 = (bf16[32,3584]{1,0:T(8,128)(2,1)S(1)}, bf16[32,3584]{1,0:T(8,128)(2,1)S(1)}, u32[]{:S(2)}, u32[]{:S(2)}) collective-permute-start(bf16[32,3584]{1,0:T(8,128)(2,1)S(1)} %collective-permute-done.8), channel_id=1, source_target_pairs={{0,2},{2,4},{4,6},{6,8},{8,10},{10,12},{12,14},{14,16},{16,18},{18... | collective-permute-start | bytes 688136 | tf_op jit(solution)/shard_map/ppermute | solution.py:47
  113.1 9.6 %collective-permute-start.10 = (bf16[32,3584]{1,0:T(8,128)(2,1)S(1)}, bf16[32,3584]{1,0:T(8,128)(2,1)S(1)}, u32[]{:S(2)}, u32[]{:S(2)}) collective-permute-start(bf16[32,3584]{1,0:T(8,128)(2,1)S(1)} %collective-permute-done.9), channel_id=1, source_target_pairs={{0,2},{2,4},{4,6},{6,8},{8,10},{10,12},{12,14},{14,16},{16,18},{18... | collective-permute-start | bytes 688136 | tf_op jit(solution)/shard_map/ppermute | solution.py:47
  122.8 9.6 %collective-permute-start.11 = (bf16[32,3584]{1,0:T(8,128)(2,1)S(1)}, bf16[32,3584]{1,0:T(8,128)(2,1)S(1)}, u32[]{:S(2)}, u32[]{:S(2)}) collective-permute-start(bf16[32,3584]{1,0:T(8,128)(2,1)S(1)} %collective-permute-done.10), channel_id=1, source_target_pairs={{0,2},{2,4},{4,6},{6,8},{8,10},{10,12},{12,14},{14,16},{16,18},{18... | collective-permute-start | bytes 688136 | tf_op jit(solution)/shard_map/ppermute | solution.py:47
  132.4 9.6 %collective-permute-start.12 = (bf16[32,3584]{1,0:T(8,128)(2,1)S(1)}, bf16[32,3584]{1,0:T(8,128)(2,1)S(1)}, u32[]{:S(2)}, u32[]{:S(2)}) collective-permute-start(bf16[32,3584]{1,0:T(8,128)(2,1)S(1)} %collective-permute-done.11), channel_id=1, source_target_pairs={{0,2},{2,4},{4,6},{6,8},{8,10},{10,12},{12,14},{14,16},{16,18},{18... | collective-permute-start | bytes 688136 | tf_op jit(solution)/shard_map/ppermute | solution.py:47
  142.0 9.7 %collective-permute-start.13 = (bf16[32,3584]{1,0:T(8,128)(2,1)S(1)}, bf16[32,3584]{1,0:T(8,128)(2,1)}, u32[]{:S(2)}, u32[]{:S(2)}) collective-permute-start(bf16[32,3584]{1,0:T(8,128)(2,1)S(1)} %collective-permute-done.12), channel_id=1, source_target_pairs={{0,2},{2,4},{4,6},{6,8},{8,10},{10,12},{12,14},{14,16},{16,18},{18... | collective-permute-start | bytes 688136 | tf_op jit(solution)/shard_map/ppermute | solution.py:47
  151.7 24.3 %collective-permute-start.14 = (bf16[32,3584]{1,0:T(8,128)(2,1)}, bf16[32,3584]{1,0:T(8,128)(2,1)}, u32[]{:S(2)}, u32[]{:S(2)}) collective-permute-start(bf16[32,3584]{1,0:T(8,128)(2,1)} %collective-permute-done.13), channel_id=1, source_target_pairs={{0,2},{2,4},{4,6},{6,8},{8,10},{10,12},{12,14},{14,16},{16,18},{18... | collective-permute-start | bytes 688136 | tf_op jit(solution)/shard_map/ppermute | solution.py:47
  229.7 45.3 %all-gather.4.cloned.1.call-start = ((), (), s32[]{:S(2)}) async-start(), calls=%async_computation.4 | async-start | bytes 3538944 | tf_op jit(solution)/shard_map/all_gather | solution.py:65
  252.6 195.5 %reduce-scatter.6.cloned.1.call-start = ((), (), s32[]{:S(2)}) async-start(), calls=%async_computation.5 | async-start | bytes 7798784 | tf_op jit(solution)/shard_map/reduce_scatter | solution.py:74
  289.9 235.5 %all-gather.6.cloned.1.call-start = ((), (), s32[]{:S(2)}) async-start(), calls=%async_computation.6 | async-start | bytes 3899392 | tf_op jit(solution)/shard_map/all_gather | solution.py:80
  450.6 94.4 %reduce-scatter.8.cloned.1.call-start = ((), (), s32[]{:S(2)}) async-start(), calls=%async_computation.7 | async-start | bytes 3538944 | tf_op jit(solution)/shard_map/reduce_scatter | solution.py:86
  536.2 62.7 %all-gather.8.cloned.1.call-start = ((), (), s32[]{:S(2)}) async-start(), calls=%async_computation.8 | async-start | bytes 3538944 | tf_op jit(solution)/shard_map/all_gather | solution.py:92
  (15 other events, 491.9 us)
Sparse Core Ops, SparseCore 0:
  229.8 18.5 reduce-scatter.3
  252.7 12.2 all-gather.3
  290.0 158.0 reduce-scatter.5
  451.3 73.9 all-gather.5
  536.3 8.6 reduce-scatter.7
  548.8 12.2 all-gather.7
